TPU v7x, 256 devices: a whole 4x4x8 slice. The times are simulated.
256 devices in a mesh: px: 32 (over z, x), py: 8 (over y, core).
Axes of the slice: x: 4, y: 4, z: 8, core: 2. Of those that a mesh axis runs over, the one named last changes fastest.
Arguments:
- counts: int32 [32], replicated, may hold values from 1 to 6, 64 in all
- coefficient: float32 [192, 8, 4096], P('px', 'py'), may hold values from 0.2 to 5
- signs: int32 [192, 8, 4096], P('px', 'py'), may hold values from 0 to 1
- basis_old: float32 [192, 8, 16, 4096], P('px', 'py'), may hold values from -8 to 8
- basis_last: float32 [192, 8, 16, 4096], P('px', 'py'), may hold values from -8 to 8
- residual_factor: float32 [16, 16], replicated, may hold values from -12 to 12
- previous_coef: float32 [32, 16], replicated, may hold values from -12 to 12
- sample_rows: int32 [2048], replicated, may hold values from 0 to 2097151, as said below
Outputs:
- new_block: float32 [192, 8, 16, 4096], P('px', 'py')
- sketch: float32 [48, 2048], P(None, ('px', 'py'))
- solution: float32 [32, 16], replicated
Inputs may be any that keep to these rules, and one draw needn't show every extreme that they name: Index i of px owns counts[i] consecutive patch columns, in px order; the largest count is exactly 6. `sample_rows`: distinct cell numbers, among them 0 and 2097151.
All inputs are finite; a program needn't handle non-finite values.
Results may differ from a plain program's by a relative error of at most 0.0003.
Values sent between devices are 32-bit elements; how exact they have to be, the bound alone decides.
No kernel may reach another device: no remote copies, remote signals or barrier semaphores. Data moves between devices by JAX's collectives and lax.ppermute only.
A program may use at most 256 MiB of HBM per device.

v0:
```python
import math
import jax
import jax.numpy as jnp
from jax import lax
from jax.sharding import PartitionSpec as P

PS = 16
K = 2048
MEANX = 2
CAP = 6
CELLS = 4096
highest = lax.Precision.HIGHEST


def extended(block, sides, width):
    for axis, dim in sides:
        count = lax.axis_size(axis)
        forward = [(i, i + 1) for i in range(count - 1)]
        backward = [(target, source) for source, target in forward]
        low = lax.ppermute(
            lax.slice_in_dim(block, block.shape[dim] - width, None, axis=dim), axis, forward
        )
        high = lax.ppermute(lax.slice_in_dim(block, 0, width, axis=dim), axis, backward)
        block = jnp.concatenate([low, block, high], axis=dim)
    return block


def parity_of(values):
    folded = values
    for amount in (16, 8, 4, 2, 1):
        folded = jnp.bitwise_xor(folded, jnp.right_shift(folded, amount))
    return jnp.bitwise_and(folded, 1)


def sign_table(length):
    indices = jnp.arange(length, dtype=jnp.int32)
    parity = parity_of(jnp.bitwise_and(indices[:, None], indices[None, :]))
    return (1 - 2 * parity).astype(jnp.float32)


def transform_cells(values):
    inner_len = min(CELLS, 128)
    outer_len = CELLS // inner_len
    shaped = values.reshape(values.shape[:-1] + (outer_len, inner_len))
    shaped = jnp.einsum("sjab,bd->sjad", shaped, sign_table(inner_len), precision=highest)
    shaped = jnp.einsum("ca,sjad->sjcd", sign_table(outer_len), shaped, precision=highest)
    return shaped.reshape(values.shape)


def shift_pair(cube_vals, low_plane, high_plane, axis_pos):
    below = jnp.concatenate(
        [
            jnp.expand_dims(low_plane, axis_pos),
            lax.slice_in_dim(cube_vals, 0, PS - 1, axis=axis_pos),
        ],
        axis=axis_pos,
    )
    above = jnp.concatenate(
        [lax.slice_in_dim(cube_vals, 1, PS, axis=axis_pos), jnp.expand_dims(high_plane, axis_pos)],
        axis=axis_pos,
    )
    return (below, above)


def apply_operator(last_local, kappa_local, held_count, slot_ids):
    channels = last_local.shape[1] + 1
    plane_size = PS * PS
    joined = jnp.concatenate([last_local, kappa_local[:, None]], axis=1)
    cube_vals = joined.reshape(CAP, channels, PS, PS, PS)
    first_face = cube_vals[0, :, 0].reshape(channels, plane_size)
    last_slot = lax.dynamic_index_in_dim(cube_vals, held_count - 1, 0, keepdims=False)
    last_face = last_slot[:, PS - 1].reshape(channels, plane_size)
    x_ghost = extended(jnp.stack([first_face, last_face]), (("px", 0),), 1)
    y_planes = jnp.stack([cube_vals[:, :, :, 0], cube_vals[:, :, :, PS - 1]]).reshape(
        2, CAP, channels, plane_size
    )
    y_ghost = extended(y_planes, (("py", 0),), 1)
    ghost_low = x_ghost[0].reshape(channels, PS, PS)
    ghost_high = x_ghost[3].reshape(channels, PS, PS)
    x_low = jnp.concatenate([ghost_low[None], cube_vals[:-1, :, PS - 1]], axis=0)
    next_faces = jnp.concatenate([cube_vals[1:, :, 0], jnp.zeros_like(cube_vals[:1, :, 0])], axis=0)
    x_high = jnp.where(
        (slot_ids == held_count - 1)[:, None, None, None], ghost_high[None], next_faces
    )
    y_low = y_ghost[0].reshape(CAP, channels, PS, PS)
    y_high = y_ghost[3].reshape(CAP, channels, PS, PS)
    z_zero = jnp.zeros((CAP, channels, PS, PS), jnp.float32)
    centre_vals = cube_vals[:, :-1]
    centre_kappa = cube_vals[:, -1:]
    diag_sum = jnp.zeros_like(centre_kappa)
    weighted = jnp.zeros_like(centre_vals)
    for low_plane, high_plane, axis_pos in (
        (x_low, x_high, 2),
        (y_low, y_high, 3),
        (z_zero, z_zero, 4),
    ):
        kappa_pair = shift_pair(centre_kappa, low_plane[:, -1:], high_plane[:, -1:], axis_pos)
        value_pair = shift_pair(centre_vals, low_plane[:, :-1], high_plane[:, :-1], axis_pos)
        for near_kappa, near_vals in zip(kappa_pair, value_pair):
            weight = 0.5 * (centre_kappa + near_kappa)
            diag_sum = diag_sum + weight
            weighted = weighted + weight * near_vals
    summed = diag_sum * centre_vals - weighted
    return summed.reshape(CAP, channels - 1, CELLS)


def normal_parts(sketch_cols, proj_coef, previous_coef, residual_factor):
    pair_count = proj_coef.shape[0]
    width_rhs = proj_coef.shape[1]
    pair_rows = sketch_cols[:pair_count]
    first_image = jnp.einsum("ab,ak->bk", previous_coef, pair_rows, precision=highest)
    second_image = (
        jnp.einsum("ab,ak->bk", proj_coef, pair_rows, precision=highest) + sketch_cols[pair_count:]
    )
    images = jnp.concatenate([first_image, second_image], axis=0)
    target = jnp.einsum("ab,ak->bk", residual_factor, sketch_cols[:width_rhs], precision=highest)
    return (
        jnp.dot(images, images.T, precision=highest),
        jnp.dot(images, target.T, precision=highest),
    )


def solve_normal(normal_gram, normal_cross):
    factor_low = jnp.linalg.cholesky(normal_gram)
    middle = lax.linalg.triangular_solve(factor_low, normal_cross, left_side=True, lower=True)
    return lax.linalg.triangular_solve(
        factor_low, middle, left_side=True, lower=True, transpose_a=True
    )


def body(
    counts, coefficient, signs, basis_old, basis_last, residual_factor, previous_coef, sample_rows
):
    px_index = lax.axis_index("px")
    py_index = lax.axis_index("py")
    py_count = lax.axis_size("py")
    device_count = lax.axis_size("px") * py_count
    total_cells = MEANX * device_count * CELLS
    offsets = jnp.cumsum(counts) - counts
    held_count = counts[px_index]
    slot_ids = jnp.arange(CAP, dtype=jnp.int32)
    live_weight = (slot_ids < held_count).astype(jnp.float32)
    old_local = basis_old[:, 0] * live_weight[:, None, None]
    last_local = basis_last[:, 0] * live_weight[:, None, None]
    image = (
        apply_operator(last_local, coefficient[:, 0], held_count, slot_ids)
        * live_weight[:, None, None]
    )
    pair = jnp.concatenate([old_local, last_local], axis=1)
    local_gram = jnp.einsum("sac,sbc->ab", pair, image, precision=highest)
    patch_ids = (offsets[px_index] + slot_ids) * py_count + py_index
    sign_flips = (1 - 2 * signs[:, 0]).astype(jnp.float32)
    share_width = K // device_count
    share_start = (px_index * py_count + py_index) * share_width
    proj_coef = lax.psum(local_gram, ("px", "py")) / total_cells
    new_local = image - jnp.einsum("sac,ab->sbc", pair, proj_coef, precision=highest)
    spread = transform_cells(jnp.concatenate([pair, new_local], axis=1) * sign_flips[:, None, :])
    picked = jnp.take(spread, sample_rows % CELLS, axis=2)
    parity = parity_of(jnp.bitwise_and(patch_ids[:, None], (sample_rows // CELLS)[None, :]))
    weights = (1 - 2 * parity).astype(jnp.float32) * live_weight[:, None]
    partial_value = jnp.einsum("sk,sjk->jk", weights, picked, precision=highest) * (
        1.0 / math.sqrt(total_cells)
    )
    sketch_whole = lax.psum(partial_value, ("px", "py"))
    sketch_mine = lax.dynamic_slice_in_dim(sketch_whole, share_start, share_width, 1)
    normal_gram, normal_cross = normal_parts(
        sketch_whole, proj_coef, previous_coef, residual_factor
    )
    solution = solve_normal(normal_gram, normal_cross)
    return (new_local[:, None], sketch_mine, solution)


def solution(mesh):
    in_specs = (
        P(),
        P("px", "py", None),
        P("px", "py", None),
        P("px", "py", None, None),
        P("px", "py", None, None),
        P(),
        P(),
        P(),
    )
    out_specs = (P("px", "py", None, None), P(None, ("px", "py")), P())
    return jax.shard_map(body, mesh=mesh, in_specs=in_specs, out_specs=out_specs, check_vma=False)
```

profile of v0, /device:TPU:1, one launch (start us, length us, event | category | flops | bytes accessed | tf_op | source)
XLA Modules:
  0.0 603.8 jit_solution(3196232569332509484)
XLA Ops:
  7.2 1.2 dynamic_slice.13
  9.1 2.3 bitcast_multiply_fusion.2
  11.7 2.4 copy.21
  14.0 8.6 %reshape.92 = f32[6,17,16,16,16]{4,3,2,0,1:T(8,128)} reshape(f32[6,17,4096]{2,0,1:T(8,128)} %copy.21) | data formatting | bytes 3342336 | tf_op jit(solution)/shard_map/reshape | solution.py:69
  22.6 0.9 slice.167
  23.7 1.3 collective-permute-start.1
  26.3 3.2 constant_dynamic-slice_fusion.1
  29.5 3.9 copy.22
  33.3 0.9 slice.163
  34.3 5.2 collective-permute-start
  39.5 10.8 %slice_reduce_fusion = (f32[6,17,16,16]{3,2,0,1:T(8,128)}, f32[6,17,16,16]{3,2,0,1:T(8,128)}) fusion(f32[6,17,16,16,16]{4,3,2,0,1:T(8,128)} %reshape.92), kind=kLoop, calls=%fused_computation.34 | loop fusion | bytes 417792 | tf_op jit(solution)/shard_map/slice | solution.py:74
  50.2 1.5 reshape.112
  51.7 0.8 copy.47
  52.5 4.6 collective-permute-start.2
  57.1 1.5 reshape.113
  58.6 0.8 copy.48
  59.3 3.0 collective-permute-start.3
  62.4 17.5 %fusion.102 = (f32[6,16,15,16,16]{4,3,2,0,1:T(8,128)}, f32[6,16,15,16,16]{4,3,2,0,1:T(8,128)}) fusion(f32[6,17,16,16,16]{4,3,2,0,1:T(8,128)} %reshape.92), kind=kLoop, calls=%fused_computation.173 | loop fusion | bytes 5898240 | tf_op jit(solution)/shard_map/slice | solution.py:59
  79.8 1.2 slice_bitcast_fusion.1
  81.1 9.2 %fusion.101 = (f32[6,16,16,15,16]{4,3,2,0,1:T(8,128)}, f32[6,16,16,15,16]{4,3,2,0,1:T(8,128)}) fusion(f32[6,17,16,16,16]{4,3,2,0,1:T(8,128)S(1)} %bitcast.139), kind=kLoop, calls=%fused_computation.172 | loop fusion | bytes 5898240 | tf_op jit(solution)/shard_map/slice | solution.py:59
  90.3 9.8 %fusion.100 = (f32[6,16,16,16,15]{4,3,2,0,1:T(8,128)}, f32[6,16,16,16,15]{4,3,2,0,1:T(8,128)}) fusion(f32[6,17,16,16,16]{4,3,2,0,1:T(8,128)S(1)} %bitcast.139), kind=kLoop, calls=%fused_computation.171 | loop fusion | bytes 5898240 | tf_op jit(solution)/shard_map/slice | solution.py:54
  100.1 1.4 fusion.99
  101.5 1.2 fusion.97
  102.8 1.3 fusion.98
  105.3 1.4 copy.54
  106.7 1.4 copy.55
  109.1 4.0 bitcast_multiply_fusion.1
  114.3 1.3 copy.53
  115.8 0.8 reduce.7
  116.7 1.3 pad_select_fusion
  118.1 0.8 slice_bitcast_fusion.3
  118.9 3.5 fusion.30
  122.4 1.3 slice_bitcast_fusion
  123.7 0.9 copy.31
  124.6 1.2 reshape_squeeze.7
  125.8 2.1 slice.185
  127.9 1.4 slice.175
  129.3 0.9 copy.29
  130.2 1.2 reshape_squeeze.6
  131.4 2.1 slice.182
  133.5 0.8 slice.171
  134.3 5.0 add_bitcast_fusion
  139.3 37.8 %fusion = f32[6,16,16,16,16]{4,3,2,0,1:T(8,128)} fusion(f32[6,17,16,16,16]{4,3,2,0,1:T(8,128)} %reshape.92, f32[6,16,15,16,16]{4,3,2,0,1:T(8,128)} %get-tuple-element.29, f32[6,16,1,16,16]{4,3,2,0,1:T(8,128)} %get-tuple-element.41, f32[6,16,1,16,16]{4,3,2,0,1:T(8,128)} %get-tuple-element.40, f32[6,16,15,16,16]{4,3,2,0,1:T(8,128)} %get-tuple-element.28, ...), kind=kLoop, calls=%fused_computation.2 | loop fusion | flops 6684672 | bytes 13074432 | tf_op jit(solution)/shard_map/sub | solution.py:103
  177.1 10.5 %reshape.114 = f32[6,16,4096]{2,0,1:T(8,128)} reshape(f32[6,16,16,16,16]{4,3,2,0,1:T(8,128)} %fusion) | data formatting | bytes 3145728 | tf_op jit(solution)/shard_map/reshape | solution.py:104
  187.6 4.7 fusion.14
  192.3 80.0 %psum.14 = f32[32,16]{0,1:T(8,128)S(1)} all-reduce(f32[32,16]{0,1:T(8,128)S(1)} %fusion.14), channel_id=1, replica_groups=mesh['px'=32,'py'=8] {'px','py'}, use_global_device_ids=true, to_apply=%region_0.0 | all-reduce | flops 512 | bytes 4096 | tf_op jit(solution)/shard_map/psum | solution.py:155
  272.4 4.1 fusion.6
  276.8 0.9 copy-done.5
  277.6 4.0 fusion.7
  281.6 5.7 convolution_bitcast_fusion.1
  287.3 9.7 %copy.50 = f32[6,48,32,128]{1,0,3,2:T(8,128)} copy(f32[6,48,32,128]{3,2,1,0:T(8,128)} %convolution_bitcast_fusion.1) | data formatting | bytes 9437184 | tf_op jit(solution)/shard_map/reshape | solution.py:47
  297.0 21.6 %gather_fusion = f32[2048,6,48]{2,1,0:T(8,128)} fusion(f32[6,48,4096]{1,0,2:T(8,128)} %bitcast.140, s32[2048]{0:T(1024)S(1)} %copy-done.10), kind=kCustom, calls=%fused_computation | custom fusion | bytes 4726784 | tf_op jit(solution)/shard_map/jit(_take)/gather | solution.py:158
  318.6 13.2 %multiply_reduce_fusion = f32[2048,48]{1,0:T(8,128)S(1)} fusion(f32[2048,6,48]{2,1,0:T(8,128)} %gather_fusion, f32[2048,6]{1,0:T(8,128)S(1)} %copy-done.7, pred[2048]{0:T(1024)(128)(4,1)S(1)} %copy-done.15), kind=kLoop, calls=%fused_computation.12 | loop fusion | flops 1671168 | bytes 2803712
  332.2 0.8 multiply_bitcast_fusion
  333.0 248.0 %all-reduce.7.cloned.1.call-done = f32[48,2048]{1,0:T(8,128)} async-done(((f32[48,2048]{1,0:T(8,128)}), f32[48,2048]{1,0:T(8,128)}) %all-reduce.7.cloned.1.call-update) | async-done | bytes 393232 | tf_op jit(solution)/shard_map/psum | solution.py:164
  581.0 0.8 constant_dynamic-slice_fusion
  581.8 0.7 copy.37
  582.5 1.2 convolution_add_fusion
  583.7 1.2 convolution_bitcast_fusion.2
  585.3 2.7 fusion.27
  588.1 0.7 fusion.23
  588.8 2.9 cholesky.16
  593.0 2.4 custom-call.8
  595.7 0.8 fusion.60
  (75 shorter events, 7.4 us)
Async XLA Ops:
  7.2 576.6 %copy-start = (f32[32,16]{0,1:T(8,128)S(1)}, f32[32,16]{0,1:T(8,128)}, u32[]{:S(2)}) copy-start(f32[32,16]{0,1:T(8,128)} %param.14) | copy-start | bytes 6148
  7.2 4.3 copy-start.9
  7.2 573.8 %all-reduce.7.cloned.1.call-start = ((), (), s32[]{:S(2)}) async-start(), calls=%async_computation | async-start | bytes 786432 | tf_op jit(solution)/shard_map/psum | solution.py:164
  9.1 104.6 %copy-start.12 = (f32[6]{0:T(128)}, f32[6]{0:T(128)S(1)}, u32[]{:S(2)}) copy-start(f32[6]{0:T(128)S(1)} %compare_convert_fusion) | copy-start | bytes 76
  23.7 92.0 %collective-permute-start.1 = (f32[1,17,256]{2,0,1:T(1,128)S(1)}, f32[1,17,256]{2,0,1:T(1,128)S(1)}, u32[]{:S(2)}, u32[]{:S(2)}) collective-permute-start(f32[1,17,256]{2,0,1:T(1,128)S(1)} %stack_reshape_squeeze.7), channel_id=1, source_target_pairs={{8,0},{16,8},{24,16},{32,24},{40,32},{48,40},{56,48},{64,56},{72,6... | collective-permute-start | bytes 52232 | tf_op jit(solution)/shard_map/ppermute | solution.py:23
  34.3 81.5 %collective-permute-start = (f32[1,17,256]{2,0,1:T(1,128)S(1)}, f32[1,17,256]{2,0,1:T(1,128)}, u32[]{:S(2)}, u32[]{:S(2)}) collective-permute-start(f32[1,17,256]{2,0,1:T(1,128)S(1)} %copy.46), channel_id=1, source_target_pairs={{0,8},{8,16},{16,24},{24,32},{32,40},{40,48},{48,56},{56,64},{64,7... | collective-permute-start | bytes 52232 | tf_op jit(solution)/shard_map/ppermute | solution.py:20
  52.5 76.8 %collective-permute-start.2 = (f32[1,6,17,256]{3,0,2,1:T(1,128)}, f32[1,6,17,256]{3,0,2,1:T(1,128)}, u32[]{:S(2)}, u32[]{:S(2)}) collective-permute-start(f32[1,6,17,256]{3,0,2,1:T(1,128)} %copy.47), channel_id=1, source_target_pairs={{0,1},{1,2},{2,3},{3,4},{4,5},{5,6},{6,7},{8,9},{9,10},{10,11},{11... | collective-permute-start | bytes 313352 | tf_op jit(solution)/shard_map/ppermute | solution.py:20
  58.6 21.2 %slice-start = ((s8[13369344]{0:T(1024)(128)(4,1)}), s8[4194304]{0:T(1024)(128)(4,1)S(1)}, s32[]{:S(2)}) async-start(s8[13369344]{0:T(1024)(128)(4,1)} %bitcast.138), calls=%async_computation.1 | async-start | bytes 8388608
  59.3 20.5 %slice-start.1 = ((s8[13369344]{0:T(1024)(128)(4,1)}), s8[4194304]{0:T(1024)(128)(4,1)S(1)}, s32[]{:S(2)}) async-start(s8[13369344]{0:T(1024)(128)(4,1)} %bitcast.138), calls=%async_computation.2 | async-start | bytes 8388608
  59.3 20.5 %slice-start.2 = ((s8[13369344]{0:T(1024)(128)(4,1)}), s8[4194304]{0:T(1024)(128)(4,1)S(1)}, s32[]{:S(2)}) async-start(s8[13369344]{0:T(1024)(128)(4,1)} %bitcast.138), calls=%async_computation.3 | async-start | bytes 8388608
  59.3 20.5 %slice-start.3 = ((s8[13369344]{0:T(1024)(128)(4,1)}), s8[786432]{0:T(1024)(128)(4,1)S(1)}, s32[]{:S(2)}) async-start(s8[13369344]{0:T(1024)(128)(4,1)} %bitcast.138), calls=%async_computation.4 | async-start | bytes 1572864
  59.3 64.3 %collective-permute-start.3 = (f32[1,6,17,256]{3,0,2,1:T(1,128)}, f32[1,6,17,256]{3,0,2,1:T(1,128)}, u32[]{:S(2)}, u32[]{:S(2)}) collective-permute-start(f32[1,6,17,256]{3,0,2,1:T(1,128)} %copy.48), channel_id=1, source_target_pairs={{1,0},{2,1},{3,2},{4,3},{5,4},{6,5},{7,6},{9,8},{10,9},{11,10},{12... | collective-permute-start | bytes 313352 | tf_op jit(solution)/shard_map/ppermute | solution.py:23
  100.1 3.9 copy-start.11
  100.1 5.1 copy-start.3
  101.5 5.2 copy-start.4
  102.8 5.4 copy-start.8
  102.8 5.5 copy-start.16
  116.7 5.6 copy-start.6
  177.1 10.5 %copy-start.13 = (f32[6]{0:T(128)S(1)}, f32[6]{0:T(128)}, u32[]{:S(2)}) copy-start(f32[6]{0:T(128)} %copy-done.12) | copy-start | bytes 76
  272.3 5.3 copy-start.1
  272.3 5.3 copy-start.2
  276.5 1.1 copy-start.5
  287.3 9.7 %copy-start.10 = (s32[2048]{0:T(1024)S(1)}, s32[2048]{0:T(1024)}, u32[]{:S(2)}) copy-start(s32[2048]{0:T(1024)} %get-tuple-element.33) | copy-start | bytes 24580
  297.0 21.6 %copy-start.7 = (f32[2048,6]{1,0:T(8,128)S(1)}, f32[2048,6]{1,0:T(8,128)}, u32[]{:S(2)}) copy-start(f32[2048,6]{1,0:T(8,128)} %copy.53) | copy-start | bytes 147460
  297.0 21.6 %copy-start.15 = (pred[2048]{0:T(1024)(128)(4,1)S(1)}, pred[2048]{0:T(1024)(128)(4,1)}, u32[]{:S(2)}) copy-start(pred[2048]{0:T(1024)(128)(4,1)} %compare_and_fusion) | copy-start | bytes 6148
  318.6 266.7 %copy-start.14 = (f32[16,16]{1,0:T(8,128)S(1)}, f32[16,16]{1,0:T(8,128)}, u32[]{:S(2)}) copy-start(f32[16,16]{1,0:T(8,128)} %param.13) | copy-start | bytes 3076
Sparse Core Ops, SparseCore 0:
  333.1 247.8 all-reduce.6
where the time goes:
time: 612 us; the launch traced here: 604 us
  waiting for transfers between devices  248 us (41%)
  local copies, waits for them, and re-layouts  139 us (23%)
  other arithmetic  81.1 us (13%)
  blocking collectives  80 us (13%)
  matrix products  25.8 us (4%)
  between operations  16.2 us (3%)
  starting transfers between devices  14.1 us (2%)
    psum x1, waiting for transfers between devices, body(): sketch_whole = lax.psum(partial_value, ('px', 'py'))  248 us
    psum x1, blocking collectives, body(): proj_coef = lax.psum(local_gram, ('px', 'py')) / total_cells  80 us
    sub x1, other arithmetic, apply_operator(): summed = diag_sum * centre_vals - weighted  37.8 us
    slice x2, local copies, waits for them, and re-layouts, shift_pair(): lax.slice_in_dim(cube_vals, 1, PS, axis=axis_pos)  26.7 us
    gather x1, local copies, waits for them, and re-layouts, body(): picked = jnp.take(spread, sample_rows % CELLS, axis=2)  21.6 us
    slice x4, local copies, waits for them, and re-layouts, shift_pair(): lax.slice_in_dim(cube_vals, 0, PS - 1, axis=axis_pos)  13.8 us
    unnamed x3, other arithmetic  13.3 us
  transfers between devices with their start and end apart: 5, of which 1 were waited for; matrix products, arithmetic and copies ran while one was open for 15% of the time, Pallas kernels for 0%

commit v1 on v0

--- a/solution.py
+++ b/solution.py
@@ -161,7 +161,7 @@
     partial_value = jnp.einsum("sk,sjk->jk", weights, picked, precision=highest) * (
         1.0 / math.sqrt(total_cells)
     )
-    sketch_whole = lax.psum(partial_value, ("px", "py"))
+    sketch_whole = lax.all_gather(partial_value, ("px", "py")).sum(axis=0)
     sketch_mine = lax.dynamic_slice_in_dim(sketch_whole, share_start, share_width, 1)
     normal_gram, normal_cross = normal_parts(
         sketch_whole, proj_coef, previous_coef, residual_factor

time: 612 us -> 666 us (1.088)
  other arithmetic: 81.1 us -> 112 us
  waiting for transfers between devices: 248 us -> 274 us
    all_gather x0 -> x1, waiting for transfers between devices: none -> 274 us  [body(): sketch_whole = lax.all_gather(partial_value, ('px', 'py')).sum(axis=0)]
    psum x1 -> x0, waiting for transfers between devices: 248 us -> none  [body(): sketch_whole = lax.psum(partial_value, ('px', 'py'))]
    reduce_sum x0 -> x1, other arithmetic: none -> 30.7 us  [body(): sketch_whole = lax.all_gather(partial_value, ('px', 'py')).sum(axis=0)]
  transfers between devices with their start and end apart: 5 -> 5, of which waited for: 1 -> 1; matrix products, arithmetic and copies ran while one was open for 15% -> 14% of each run, Pallas kernels for 0% -> 0%
where the time goes in v1:
time: 666 us; the launch traced here: 657 us
  waiting for transfers between devices  274 us (41%)
  local copies, waits for them, and re-layouts  138 us (21%)
  other arithmetic  112 us (17%)
  blocking collectives  80 us (12%)
  matrix products  22.9 us (3%)
  between operations  16.2 us (2%)
  starting transfers between devices  14.1 us (2%)
    all_gather x1, waiting for transfers between devices, body(): sketch_whole = lax.all_gather(partial_value, ('px', 'py')).sum(axis=0)  274 us
    psum x1, blocking collectives, body(): proj_coef = lax.psum(local_gram, ('px', 'py')) / total_cells  80 us
    sub x1, other arithmetic, apply_operator(): summed = diag_sum * centre_vals - weighted  37.8 us
    reduce_sum x1, other arithmetic, body(): sketch_whole = lax.all_gather(partial_value, ('px', 'py')).sum(axis=0)  30.7 us
    slice x2, local copies, waits for them, and re-layouts, shift_pair(): lax.slice_in_dim(cube_vals, 1, PS, axis=axis_pos)  26.7 us
    gather x1, local copies, waits for them, and re-layouts, body(): picked = jnp.take(spread, sample_rows % CELLS, axis=2)  21.6 us
    slice x4, local copies, waits for them, and re-layouts, shift_pair(): lax.slice_in_dim(cube_vals, 0, PS - 1, axis=axis_pos)  13.8 us
  transfers between devices with their start and end apart: 5, of which 1 were waited for; matrix products, arithmetic and copies ran while one was open for 14% of the time, Pallas kernels for 0%

profile of v1, /device:TPU:1, one launch (start us, length us, event | category | flops | bytes accessed | tf_op | source)
XLA Modules:
  0.0 657.1 jit_solution(306541821992453199)
XLA Ops:
  7.2 1.2 dynamic_slice.13
  8.5 0.6 compare_convert_fusion
  9.1 2.3 bitcast_multiply_fusion.2
  11.7 2.4 copy.21
  14.0 8.6 %reshape.92 = f32[6,17,16,16,16]{4,3,2,0,1:T(8,128)} reshape(f32[6,17,4096]{2,0,1:T(8,128)} %copy.21) | data formatting | bytes 3342336 | tf_op jit(solution)/shard_map/reshape | solution.py:69
  22.6 0.9 slice.167
  23.7 1.3 collective-permute-start.1
  26.3 3.2 constant_dynamic-slice_fusion.1
  29.5 3.9 copy.22
  33.3 0.9 slice.163
  34.3 5.2 collective-permute-start
  39.5 10.8 %slice_reduce_fusion = (f32[6,17,16,16]{3,2,0,1:T(8,128)}, f32[6,17,16,16]{3,2,0,1:T(8,128)}) fusion(f32[6,17,16,16,16]{4,3,2,0,1:T(8,128)} %reshape.92), kind=kLoop, calls=%fused_computation.34 | loop fusion | bytes 417792 | tf_op jit(solution)/shard_map/slice | solution.py:74
  50.2 1.5 reshape.113
  51.7 0.8 copy.47
  52.5 4.6 collective-permute-start.2
  57.1 1.5 reshape.114
  58.6 0.8 copy.48
  59.3 3.0 collective-permute-start.3
  62.4 17.5 %fusion.102 = (f32[6,16,15,16,16]{4,3,2,0,1:T(8,128)}, f32[6,16,15,16,16]{4,3,2,0,1:T(8,128)}) fusion(f32[6,17,16,16,16]{4,3,2,0,1:T(8,128)} %reshape.92), kind=kLoop, calls=%fused_computation.173 | loop fusion | bytes 5898240 | tf_op jit(solution)/shard_map/slice | solution.py:59
  79.8 1.2 slice_bitcast_fusion.1
  81.1 9.2 %fusion.101 = (f32[6,16,16,15,16]{4,3,2,0,1:T(8,128)}, f32[6,16,16,15,16]{4,3,2,0,1:T(8,128)}) fusion(f32[6,17,16,16,16]{4,3,2,0,1:T(8,128)S(1)} %bitcast.140), kind=kLoop, calls=%fused_computation.172 | loop fusion | bytes 5898240 | tf_op jit(solution)/shard_map/slice | solution.py:59
  90.3 9.8 %fusion.100 = (f32[6,16,16,16,15]{4,3,2,0,1:T(8,128)}, f32[6,16,16,16,15]{4,3,2,0,1:T(8,128)}) fusion(f32[6,17,16,16,16]{4,3,2,0,1:T(8,128)S(1)} %bitcast.140), kind=kLoop, calls=%fused_computation.171 | loop fusion | bytes 5898240 | tf_op jit(solution)/shard_map/slice | solution.py:54
  100.1 1.4 fusion.99
  101.5 1.2 fusion.97
  102.8 1.3 fusion.98
  105.3 1.4 copy.54
  106.7 1.4 copy.55
  109.1 4.0 bitcast_multiply_fusion.1
  114.3 1.3 copy.53
  115.8 0.8 reduce.7
  116.7 1.3 pad_select_fusion
  118.1 0.8 slice_bitcast_fusion.3
  118.9 3.5 fusion.30
  122.4 1.3 slice_bitcast_fusion
  123.7 0.9 copy.31
  124.6 1.2 reshape_squeeze.7
  125.8 2.1 slice.185
  127.9 1.4 slice.175
  129.3 0.9 copy.29
  130.2 1.2 reshape_squeeze.6
  131.4 2.1 slice.182
  133.5 0.8 slice.171
  134.3 5.0 add_bitcast_fusion
  139.3 37.8 %fusion = f32[6,16,16,16,16]{4,3,2,0,1:T(8,128)} fusion(f32[6,17,16,16,16]{4,3,2,0,1:T(8,128)} %reshape.92, f32[6,16,15,16,16]{4,3,2,0,1:T(8,128)} %get-tuple-element.29, f32[6,16,1,16,16]{4,3,2,0,1:T(8,128)} %get-tuple-element.41, f32[6,16,1,16,16]{4,3,2,0,1:T(8,128)} %get-tuple-element.40, f32[6,16,15,16,16]{4,3,2,0,1:T(8,128)} %get-tuple-element.28, ...), kind=kLoop, calls=%fused_computation.2 | loop fusion | flops 6684672 | bytes 13074432 | tf_op jit(solution)/shard_map/sub | solution.py:103
  177.1 10.5 %reshape.115 = f32[6,16,4096]{2,0,1:T(8,128)} reshape(f32[6,16,16,16,16]{4,3,2,0,1:T(8,128)} %fusion) | data formatting | bytes 3145728 | tf_op jit(solution)/shard_map/reshape | solution.py:104
  187.6 4.7 fusion.14
  192.3 80.0 %psum.7 = f32[32,16]{0,1:T(8,128)S(1)} all-reduce(f32[32,16]{0,1:T(8,128)S(1)} %fusion.14), channel_id=1, replica_groups=mesh['px'=32,'py'=8] {'px','py'}, use_global_device_ids=true, to_apply=%region_0.0 | all-reduce | flops 512 | bytes 4096 | tf_op jit(solution)/shard_map/psum | solution.py:155
  272.4 4.1 fusion.6
  276.8 0.9 copy-done.5
  277.6 4.0 fusion.7
  281.6 5.7 convolution_bitcast_fusion.1
  287.3 9.7 %copy.50 = f32[6,48,32,128]{1,0,3,2:T(8,128)} copy(f32[6,48,32,128]{3,2,1,0:T(8,128)} %convolution_bitcast_fusion.1) | data formatting | bytes 9437184 | tf_op jit(solution)/shard_map/reshape | solution.py:47
  297.0 21.6 %gather_fusion = f32[2048,6,48]{2,1,0:T(8,128)} fusion(f32[6,48,4096]{1,0,2:T(8,128)} %bitcast.141, s32[2048]{0:T(1024)S(1)} %copy-done.10), kind=kCustom, calls=%fused_computation | custom fusion | bytes 4726784 | tf_op jit(solution)/shard_map/jit(_take)/gather | solution.py:158
  318.6 13.2 %multiply_reduce_fusion = f32[2048,48]{1,0:T(8,128)S(1)} fusion(f32[2048,6,48]{2,1,0:T(8,128)} %gather_fusion, f32[2048,6]{1,0:T(8,128)S(1)} %copy-done.7, pred[2048]{0:T(1024)(128)(4,1)S(1)} %copy-done.15), kind=kLoop, calls=%fused_computation.12 | loop fusion | flops 1671168 | bytes 2803712
  332.2 0.8 multiply_bitcast_fusion
  333.0 274.2 %all-gather.3.cloned.1.call-done = f32[12288,2048]{1,0:T(8,128)} async-done(((f32[48,2048]{1,0:T(8,128)}), f32[12288,2048]{1,0:T(8,128)}) %all-gather.3.cloned.1.call-update) | async-done | bytes 100663312 | tf_op jit(solution)/shard_map/all_gather | solution.py:164
  607.2 30.7 %reduce_sum.9 = f32[48,2048]{1,0:T(8,128)S(1)} reduce(f32[256,48,2048]{2,1,0:T(8,128)} %bitcast.43, f32[]{:T(128)} %constant.128.clone.1), dimensions={0}, to_apply=%region_2.3 | reduce | flops 25067520 | bytes 101056512 | tf_op jit(solution)/shard_map/reduce_sum | solution.py:164
  638.2 0.7 copy.37
  638.9 1.8 fusion.27
  641.4 0.7 fusion.23
  642.1 2.9 cholesky.16
  645.7 0.7 fusion.53
  646.4 2.4 custom-call.8
  649.1 0.8 fusion.60
  (76 shorter events, 6.7 us)
Async XLA Ops:
  7.2 631.7 %copy-start = (f32[16,16]{1,0:T(8,128)S(1)}, f32[16,16]{1,0:T(8,128)}, u32[]{:S(2)}) copy-start(f32[16,16]{1,0:T(8,128)} %param.13) | copy-start | bytes 3076
  7.2 4.3 copy-start.9
  7.2 600.0 %all-gather.3.cloned.1.call-start = ((), (), s32[]{:S(2)}) async-start(), calls=%async_computation | async-start | bytes 101056512 | tf_op jit(solution)/shard_map/all_gather | solution.py:164
  9.1 104.6 %copy-start.12 = (f32[6]{0:T(128)}, f32[6]{0:T(128)S(1)}, u32[]{:S(2)}) copy-start(f32[6]{0:T(128)S(1)} %compare_convert_fusion) | copy-start | bytes 76
  23.7 92.0 %collective-permute-start.1 = (f32[1,17,256]{2,0,1:T(1,128)S(1)}, f32[1,17,256]{2,0,1:T(1,128)S(1)}, u32[]{:S(2)}, u32[]{:S(2)}) collective-permute-start(f32[1,17,256]{2,0,1:T(1,128)S(1)} %stack_reshape_squeeze.7), channel_id=1, source_target_pairs={{8,0},{16,8},{24,16},{32,24},{40,32},{48,40},{56,48},{64,56},{72,6... | collective-permute-start | bytes 52232 | tf_op jit(solution)/shard_map/ppermute | solution.py:23
  34.3 81.5 %collective-permute-start = (f32[1,17,256]{2,0,1:T(1,128)S(1)}, f32[1,17,256]{2,0,1:T(1,128)}, u32[]{:S(2)}, u32[]{:S(2)}) collective-permute-start(f32[1,17,256]{2,0,1:T(1,128)S(1)} %copy.46), channel_id=1, source_target_pairs={{0,8},{8,16},{16,24},{24,32},{32,40},{40,48},{48,56},{56,64},{64,7... | collective-permute-start | bytes 52232 | tf_op jit(solution)/shard_map/ppermute | solution.py:20
  52.5 76.8 %collective-permute-start.2 = (f32[1,6,17,256]{3,0,2,1:T(1,128)}, f32[1,6,17,256]{3,0,2,1:T(1,128)}, u32[]{:S(2)}, u32[]{:S(2)}) collective-permute-start(f32[1,6,17,256]{3,0,2,1:T(1,128)} %copy.47), channel_id=1, source_target_pairs={{0,1},{1,2},{2,3},{3,4},{4,5},{5,6},{6,7},{8,9},{9,10},{10,11},{11... | collective-permute-start | bytes 313352 | tf_op jit(solution)/shard_map/ppermute | solution.py:20
  58.6 21.2 %slice-start = ((s8[13369344]{0:T(1024)(128)(4,1)}), s8[4194304]{0:T(1024)(128)(4,1)S(1)}, s32[]{:S(2)}) async-start(s8[13369344]{0:T(1024)(128)(4,1)} %bitcast.139), calls=%async_computation.1 | async-start | bytes 8388608
  59.3 20.5 %slice-start.1 = ((s8[13369344]{0:T(1024)(128)(4,1)}), s8[4194304]{0:T(1024)(128)(4,1)S(1)}, s32[]{:S(2)}) async-start(s8[13369344]{0:T(1024)(128)(4,1)} %bitcast.139), calls=%async_computation.2 | async-start | bytes 8388608
  59.3 20.5 %slice-start.2 = ((s8[13369344]{0:T(1024)(128)(4,1)}), s8[4194304]{0:T(1024)(128)(4,1)S(1)}, s32[]{:S(2)}) async-start(s8[13369344]{0:T(1024)(128)(4,1)} %bitcast.139), calls=%async_computation.3 | async-start | bytes 8388608
  59.3 20.5 %slice-start.3 = ((s8[13369344]{0:T(1024)(128)(4,1)}), s8[786432]{0:T(1024)(128)(4,1)S(1)}, s32[]{:S(2)}) async-start(s8[13369344]{0:T(1024)(128)(4,1)} %bitcast.139), calls=%async_computation.4 | async-start | bytes 1572864
  59.3 64.3 %collective-permute-start.3 = (f32[1,6,17,256]{3,0,2,1:T(1,128)}, f32[1,6,17,256]{3,0,2,1:T(1,128)}, u32[]{:S(2)}, u32[]{:S(2)}) collective-permute-start(f32[1,6,17,256]{3,0,2,1:T(1,128)} %copy.48), channel_id=1, source_target_pairs={{1,0},{2,1},{3,2},{4,3},{5,4},{6,5},{7,6},{9,8},{10,9},{11,10},{12... | collective-permute-start | bytes 313352 | tf_op jit(solution)/shard_map/ppermute | solution.py:23
  100.1 3.9 copy-start.11
  100.1 5.1 copy-start.3
  101.5 5.2 copy-start.4
  102.8 5.4 copy-start.8
  102.8 5.5 copy-start.16
  116.7 5.6 copy-start.6
  177.1 10.5 %copy-start.13 = (f32[6]{0:T(128)S(1)}, f32[6]{0:T(128)}, u32[]{:S(2)}) copy-start(f32[6]{0:T(128)} %copy-done.12) | copy-start | bytes 76
  272.3 5.3 copy-start.1
  272.3 5.3 copy-start.2
  276.5 1.1 copy-start.5
  287.3 9.7 %copy-start.10 = (s32[2048]{0:T(1024)S(1)}, s32[2048]{0:T(1024)}, u32[]{:S(2)}) copy-start(s32[2048]{0:T(1024)} %get-tuple-element.33) | copy-start | bytes 24580
  297.0 21.6 %copy-start.7 = (f32[2048,6]{1,0:T(8,128)S(1)}, f32[2048,6]{1,0:T(8,128)}, u32[]{:S(2)}) copy-start(f32[2048,6]{1,0:T(8,128)} %copy.53) | copy-start | bytes 147460
  297.0 21.6 %copy-start.15 = (pred[2048]{0:T(1024)(128)(4,1)S(1)}, pred[2048]{0:T(1024)(128)(4,1)}, u32[]{:S(2)}) copy-start(pred[2048]{0:T(1024)(128)(4,1)} %compare_and_fusion) | copy-start | bytes 6148
  607.2 33.5 %copy-start.14 = (f32[32,16]{0,1:T(8,128)S(1)}, f32[32,16]{0,1:T(8,128)}, u32[]{:S(2)}) copy-start(f32[32,16]{0,1:T(8,128)} %param.14) | copy-start | bytes 6148
Sparse Core Ops, SparseCore 0:
  333.1 274.0 all-gather.2
